TPU v7x, 32 devices: a whole 2x2x4 slice. The times are simulated.
32 devices in a mesh: fsdp: 4 (over y, x), ctx: 2 (over core), tp: 4 (over z).
Axes of the slice: x: 2, y: 2, z: 4, core: 2. Of those that a mesh axis runs over, the one named last changes fastest.
Arguments:
- block_input: float32 [4, 1024, 2048], P('fsdp', 'ctx'), may hold values from -6 to 6
- cotangent: float32 [4, 1024, 2048], P('fsdp', 'ctx'), may hold values from -6 to 6
- w_query: bfloat16 [2048, 2048], P(('fsdp', 'ctx'), 'tp'), may hold values from -0.125 to 0.125
- w_key: bfloat16 [2048, 512], P(('fsdp', 'ctx'), 'tp'), may hold values from -0.125 to 0.125
- w_value: bfloat16 [2048, 512], P(('fsdp', 'ctx'), 'tp'), may hold values from -0.125 to 0.125
- w_output: bfloat16 [2048, 2048], P('tp', ('fsdp', 'ctx')), may hold values from -4 to 4
- w_gate: bfloat16 [2048, 8192], P(('fsdp', 'ctx'), 'tp'), may hold values from -0.125 to 0.125
- w_up: bfloat16 [2048, 8192], P(('fsdp', 'ctx'), 'tp'), may hold values from -0.125 to 0.125
- w_down: bfloat16 [8192, 2048], P('tp', ('fsdp', 'ctx')), may hold values from -0.0625 to 0.0625
- attn_gain: bfloat16 [2048], P(('fsdp', 'ctx')), may hold values from 0.5 to 1.5
- ffn_gain: bfloat16 [2048], P(('fsdp', 'ctx')), may hold values from 0.5 to 1.5
Outputs:
- block_output: float32 [4, 1024, 2048], P('fsdp', 'ctx')
- input_grad: float32 [4, 1024, 2048], P('fsdp', 'ctx')
- grad_query: float32 [2048, 2048], P(('fsdp', 'ctx'), 'tp')
- grad_key: float32 [2048, 512], P(('fsdp', 'ctx'), 'tp')
- grad_value: float32 [2048, 512], P(('fsdp', 'ctx'), 'tp')
- grad_output: float32 [2048, 2048], P('tp', ('fsdp', 'ctx'))
- grad_gate: float32 [2048, 8192], P(('fsdp', 'ctx'), 'tp')
- grad_up: float32 [2048, 8192], P(('fsdp', 'ctx'), 'tp')
- grad_down: float32 [8192, 2048], P('tp', ('fsdp', 'ctx'))
- grad_attn_gain: float32 [2048], P(('fsdp', 'ctx'))
- grad_ffn_gain: float32 [2048], P(('fsdp', 'ctx'))
All inputs are finite; a program needn't handle non-finite values.
Results may differ from a plain program's by a relative error of at most 0.013.
Values may be sent and summed in bfloat16 or wider, within the bound.
No kernel may reach another device: no remote copies, remote signals or barrier semaphores. Data moves between devices by JAX's collectives and lax.ppermute only.
A program may use at most 256 MiB of HBM per device.

v0:
```python
import jax
import jax.numpy as jnp
from jax import lax
from jax.sharding import PartitionSpec as P

HD = 64
EPS = 1e-05
BASE = 500000.0
NEG = -1e30


def shifted(shard, axis, by):
    count = lax.axis_size(axis)
    pairs = [(i, i + by) for i in range(count) if 0 <= i + by < count]
    return lax.ppermute(shard, axis, pairs)


def rotate(values, positions, sign):
    half = values.shape[-1] // 2
    inverse = BASE ** (-(jnp.arange(half, dtype=jnp.float32) * 2.0) / values.shape[-1])
    angle = positions.astype(jnp.float32)[:, None] * inverse[None, :]
    cosine = jnp.cos(angle)[:, None, :]
    sine = sign * jnp.sin(angle)[:, None, :]
    first = values[..., :half]
    second = values[..., half:]
    return jnp.concatenate(
        [first * cosine - second * sine, second * cosine + first * sine], axis=-1
    )


def norm_forward(rows, gain):
    scale = lax.rsqrt(jnp.mean(rows * rows, axis=-1, keepdims=True) + EPS)
    return (rows * scale * gain, scale)


def norm_backward(rows, scale, gain, grad):
    weighted = grad * gain
    d_rows = scale * weighted - rows * scale**3 * jnp.mean(weighted * rows, axis=-1, keepdims=True)
    return (d_rows, jnp.sum(grad * rows * scale, axis=0))


def forward_block(queries, keys, vals, allow, scale):
    scores = jnp.einsum("gbd,kd->gbk", queries, keys, preferred_element_type=jnp.float32) * scale
    scores = jnp.where(allow[None], scores, NEG)
    top = jnp.max(scores, axis=-1, keepdims=True)
    total = top[..., 0] + jnp.log(jnp.sum(jnp.exp(scores - top), axis=-1))
    probs = jnp.exp(scores - total[..., None]).astype(jnp.bfloat16)
    out = jnp.einsum("gbk,kd->gbd", probs, vals, preferred_element_type=jnp.float32)
    return (out.astype(jnp.bfloat16), total)


def backward_block(queries, keys, vals, allow, total, grad_out, out, scale):
    scores = jnp.einsum("gbd,kd->gbk", queries, keys, preferred_element_type=jnp.float32) * scale
    scores = jnp.where(allow[None], scores, NEG)
    probs = jnp.exp(scores - total[..., None])
    rounded = probs.astype(jnp.bfloat16)
    d_vals = jnp.einsum("gbk,gbd->kd", rounded, grad_out, preferred_element_type=jnp.float32)
    d_probs = jnp.einsum("gbd,kd->gbk", grad_out, vals, preferred_element_type=jnp.float32)
    delta = jnp.sum(grad_out.astype(jnp.float32) * out.astype(jnp.float32), axis=-1)
    d_scores = (probs * (d_probs - delta[..., None]) * scale).astype(jnp.bfloat16)
    d_query = jnp.einsum("gbk,kd->gbd", d_scores, keys, preferred_element_type=jnp.float32)
    d_keys = jnp.einsum("gbk,gbd->kd", d_scores, queries, preferred_element_type=jnp.float32)
    return (d_query, d_keys, d_vals)


def split_blocks(tensor, count, block):
    return tensor.reshape((tensor.shape[0], count, block) + tensor.shape[2:]).swapaxes(0, 1)


def attention_forward(grouped, keys, vals, allow, block, scale):

    def per_head(items):
        head_q, head_k, head_v = items
        groups, rows, width = head_q.shape
        count = rows // block
        outs, totals = lax.map(
            lambda piece: forward_block(piece[0], head_k, head_v, piece[1], scale),
            (split_blocks(head_q, count, block), allow.reshape(count, block, allow.shape[1])),
        )
        return (
            outs.swapaxes(0, 1).reshape(groups, rows, width),
            totals.swapaxes(0, 1).reshape(groups, rows),
        )

    return lax.map(per_head, (grouped, keys, vals))


def attention_backward(grouped, keys, vals, allow, totals, grads, outs, block, scale):

    def per_head(items):
        head_q, head_k, head_v, head_t, head_g, head_o = items
        groups, rows, width = head_q.shape
        count = rows // block

        def step(carry, piece):
            d_query, d_keys, d_vals = backward_block(
                piece[0], head_k, head_v, piece[1], piece[2], piece[3], piece[4], scale
            )
            return ((carry[0] + d_keys, carry[1] + d_vals), d_query)

        zeros = jnp.zeros(head_k.shape, jnp.float32)
        pieces = (
            split_blocks(head_q, count, block),
            allow.reshape(count, block, allow.shape[1]),
            split_blocks(head_t, count, block),
            split_blocks(head_g, count, block),
            split_blocks(head_o, count, block),
        )
        (d_keys, d_vals), d_query = lax.scan(step, (zeros, zeros), pieces)
        return (d_query.swapaxes(0, 1).reshape(groups, rows, width), d_keys, d_vals)

    return lax.map(per_head, (grouped, keys, vals, totals, grads, outs))


def dotf(left, right):
    return jnp.dot(left, right, preferred_element_type=jnp.float32)


def body(
    block_input,
    cotangent,
    w_query,
    w_key,
    w_value,
    w_output,
    w_gate,
    w_up,
    w_down,
    attn_gain,
    ffn_gain,
):
    wq, wk, wv, wo, wg, wu, wd, gain_qa, gain_qf = (
        lax.all_gather(w_query, ("fsdp", "ctx"), axis=0, tiled=True),
        lax.all_gather(w_key, ("fsdp", "ctx"), axis=0, tiled=True),
        lax.all_gather(w_value, ("fsdp", "ctx"), axis=0, tiled=True),
        lax.all_gather(w_output, ("fsdp", "ctx"), axis=1, tiled=True),
        lax.all_gather(w_gate, ("fsdp", "ctx"), axis=0, tiled=True),
        lax.all_gather(w_up, ("fsdp", "ctx"), axis=0, tiled=True),
        lax.all_gather(w_down, ("fsdp", "ctx"), axis=1, tiled=True),
        lax.all_gather(attn_gain, ("fsdp", "ctx"), axis=0, tiled=True),
        lax.all_gather(ffn_gain, ("fsdp", "ctx"), axis=0, tiled=True),
    )
    rows = block_input[0]
    cot = cotangent[0]
    local = rows.shape[0]
    block = min(512, local)
    scale = HD ** (-0.5)
    heads = wq.shape[1] // HD
    kv_heads = wk.shape[1] // HD
    groups = heads // kv_heads
    place = lax.axis_index("ctx")
    positions = place * local + jnp.arange(local, dtype=jnp.int32)
    gain_a = gain_qa.astype(jnp.float32)
    gain_f = gain_qf.astype(jnp.float32)
    normed_f, scale_a = norm_forward(rows, gain_a)
    normed = normed_f.astype(jnp.bfloat16)
    query = dotf(normed, wq).reshape(local, heads, HD)
    keys = dotf(normed, wk).reshape(local, kv_heads, HD)
    vals = dotf(normed, wv)
    query_rot = rotate(query, positions, 1.0).astype(jnp.bfloat16)
    keys_rot = rotate(keys, positions, 1.0).astype(jnp.bfloat16).reshape(local, kv_heads * HD)
    vals_b = vals.astype(jnp.bfloat16)
    keys_prev, vals_prev = shifted((keys_rot, vals_b), "ctx", 1)
    all_keys = (
        jnp.concatenate([keys_prev, keys_rot], axis=0)
        .reshape(2 * local, kv_heads, HD)
        .transpose(1, 0, 2)
    )
    all_vals = (
        jnp.concatenate([vals_prev, vals_b], axis=0)
        .reshape(2 * local, kv_heads, HD)
        .transpose(1, 0, 2)
    )
    grouped = query_rot.reshape(local, kv_heads, groups, HD).transpose(1, 2, 0, 3)
    index = jnp.arange(local, dtype=jnp.int32)
    earlier = jnp.broadcast_to(place > 0, (local, local))
    causal = index[None, :] <= index[:, None]
    allow = jnp.concatenate([earlier, causal], axis=1)
    attn, totals = attention_forward(grouped, all_keys, all_vals, allow, block, scale)
    attn_flat = attn.transpose(2, 0, 1, 3).reshape(local, heads * HD)
    hidden = rows + lax.psum(dotf(attn_flat, wo), "tp")
    hnorm_f, scale_f = norm_forward(hidden, gain_f)
    hnorm = hnorm_f.astype(jnp.bfloat16)
    gate = dotf(hnorm, wg)
    up = dotf(hnorm, wu)
    sigma = jax.nn.sigmoid(gate)
    active = gate * sigma
    inner = (active * up).astype(jnp.bfloat16)
    out = hidden + lax.psum(dotf(inner, wd).astype(jnp.bfloat16), "tp").astype(jnp.float32)
    cot_b = cot.astype(jnp.bfloat16)
    d_inner = dotf(cot_b, wd.T)
    d_gate = (d_inner * up * sigma * (1.0 + gate * (1.0 - sigma))).astype(jnp.bfloat16)
    d_up = (d_inner * active).astype(jnp.bfloat16)
    d_hnorm = lax.psum(dotf(d_gate, wg.T) + dotf(d_up, wu.T), "tp")
    d_norm, g_ffn = norm_backward(hidden, scale_f, gain_f, d_hnorm)
    d_hidden = cot + d_norm
    dh_b = d_hidden.astype(jnp.bfloat16)
    d_attn = (
        dotf(dh_b, wo.T)
        .astype(jnp.bfloat16)
        .reshape(local, kv_heads, groups, HD)
        .transpose(1, 2, 0, 3)
    )
    d_query, d_keys, d_vals = attention_backward(
        grouped, all_keys, all_vals, allow, totals, d_attn, attn, block, scale
    )
    keys_grad = d_keys.transpose(1, 0, 2).reshape(2 * local, kv_heads * HD)
    vals_grad = d_vals.transpose(1, 0, 2).reshape(2 * local, kv_heads * HD)
    keys_back, vals_back = shifted((keys_grad[:local], vals_grad[:local]), "ctx", -1)
    keys_own = keys_grad[local:] + keys_back
    vals_own = vals_grad[local:] + vals_back
    d_query = d_query.transpose(2, 0, 1, 3).reshape(local, heads, HD)
    dq_b = rotate(d_query, positions, -1.0).astype(jnp.bfloat16).reshape(local, heads * HD)
    dk_b = (
        rotate(keys_own.reshape(local, kv_heads, HD), positions, -1.0)
        .astype(jnp.bfloat16)
        .reshape(local, kv_heads * HD)
    )
    dv_b = vals_own.astype(jnp.bfloat16)
    d_normed = lax.psum(dotf(dq_b, wq.T) + dotf(dk_b, wk.T) + dotf(dv_b, wv.T), "tp")
    d_rows, g_attn = norm_backward(rows, scale_a, gain_a, d_normed)
    d_input = d_hidden + d_rows
    s_query, s_key, s_value, s_output, s_gate, s_up, s_down, s_attn, s_ffn = (
        lax.psum_scatter(dotf(normed.T, dq_b), ("fsdp", "ctx"), scatter_dimension=0, tiled=True),
        lax.psum_scatter(dotf(normed.T, dk_b), ("fsdp", "ctx"), scatter_dimension=0, tiled=True),
        lax.psum_scatter(dotf(normed.T, dv_b), ("fsdp", "ctx"), scatter_dimension=0, tiled=True),
        lax.psum_scatter(dotf(attn_flat.T, dh_b), ("fsdp", "ctx"), scatter_dimension=1, tiled=True),
        lax.psum_scatter(dotf(hnorm.T, d_gate), ("fsdp", "ctx"), scatter_dimension=0, tiled=True),
        lax.psum_scatter(dotf(hnorm.T, d_up), ("fsdp", "ctx"), scatter_dimension=0, tiled=True),
        lax.psum_scatter(dotf(inner.T, cot_b), ("fsdp", "ctx"), scatter_dimension=1, tiled=True),
        lax.psum_scatter(g_attn, ("fsdp", "ctx"), scatter_dimension=0, tiled=True),
        lax.psum_scatter(g_ffn, ("fsdp", "ctx"), scatter_dimension=0, tiled=True),
    )
    return (
        out[None],
        d_input[None],
        s_query,
        s_key,
        s_value,
        s_output,
        s_gate,
        s_up,
        s_down,
        s_attn,
        s_ffn,
    )


def solution(mesh):
    placed = (
        P("fsdp", "ctx", None),
        P("fsdp", "ctx", None),
        P(("fsdp", "ctx"), "tp"),
        P(("fsdp", "ctx"), "tp"),
        P(("fsdp", "ctx"), "tp"),
        P("tp", ("fsdp", "ctx")),
        P(("fsdp", "ctx"), "tp"),
        P(("fsdp", "ctx"), "tp"),
        P("tp", ("fsdp", "ctx")),
        P(("fsdp", "ctx")),
        P(("fsdp", "ctx")),
    )
    return jax.shard_map(
        body,
        mesh=mesh,
        in_specs=placed,
        out_specs=(
            P("fsdp", "ctx", None),
            P("fsdp", "ctx", None),
            P(("fsdp", "ctx"), "tp"),
            P(("fsdp", "ctx"), "tp"),
            P(("fsdp", "ctx"), "tp"),
            P("tp", ("fsdp", "ctx")),
            P(("fsdp", "ctx"), "tp"),
            P(("fsdp", "ctx"), "tp"),
            P("tp", ("fsdp", "ctx")),
            P(("fsdp", "ctx")),
            P(("fsdp", "ctx")),
        ),
        check_vma=False,
    )
```

profile of v0, /device:TPU:0, one launch (start us, length us, event | category | flops | bytes accessed | tf_op | source)
XLA Modules:
  0.0 1437.5 jit_solution(5688634115593749319)
XLA Ops:
  8.6 10.4 all-gather
  19.0 10.7 all_gather.29
  30.0 3.0 fusion.52
  36.5 2.9 collective-permute-start
  39.4 8.9 all_gather.30
  51.5 2.9 collective-permute-start.1
  59.2 3.9 copy.28
  63.2 2.9 fusion.65
  66.3 12.7 while.10
  79.0 4.0 all-gather.10.cloned.1.call-done
  83.0 4.9 fusion.86
  89.7 9.1 all-gather.1
  98.8 144.2 %all-reduce.9.cloned.1.call-done = f32[512,2048]{1,0:T(8,128)} async-done(((f32[512,2048]{1,0:T(8,128)}), f32[512,2048]{1,0:T(8,128)}) %all-reduce.9.cloned.1.call-update) | async-done | bytes 4194320 | tf_op jit(solution)/shard_map/psum | solution.py:181
  243.0 4.0 multiply_reduce_fusion.2
  250.8 47.2 %all-gather.12.cloned.1.call-done = bf16[2048,2048]{1,0:T(8,128)(2,1)} async-done(((bf16[256,2048]{1,0:T(8,128)(2,1)}), bf16[2048,2048]{1,0:T(8,128)(2,1)}) %all-gather.12.cloned.1.call-update) | async-done | bytes 8388624 | tf_op jit(solution)/shard_map/all_gather | solution.py:137
  298.0 10.5 fusion.87
  308.6 45.5 %all-gather.14.cloned.1.call-done = bf16[2048,2048]{1,0:T(8,128)(2,1)} async-done(((bf16[256,2048]{1,0:T(8,128)(2,1)}), bf16[2048,2048]{1,0:T(8,128)(2,1)}) %all-gather.14.cloned.1.call-update) | async-done | bytes 8388624 | tf_op jit(solution)/shard_map/all_gather | solution.py:138
  354.1 10.5 fusion.88
  364.6 47.1 %all-gather.16.cloned.1.call-done = bf16[2048,2048]{1,0:T(8,128)(2,1)} async-done(((bf16[2048,256]{1,0:T(8,128)(2,1)}), bf16[2048,2048]{1,0:T(8,128)(2,1)}) %all-gather.16.cloned.1.call-update) | async-done | bytes 8388624 | tf_op jit(solution)/shard_map/all_gather | solution.py:139
  411.7 15.3 %multiply_convert_fusion.1 = (bf16[512,2048]{1,0:T(8,128)(2,1)S(1)}, bf16[512,2048]{1,0:T(8,128)(2,1)}, bf16[512,2048]{1,0:T(8,128)(2,1)}) fusion(f32[512,2048]{1,0:T(8,128)} %fusion.87, f32[512,2048]{1,0:T(8,128)} %fusion.88, bf16[2048,2048]{1,0:T(8,128)(2,1)} %all-gather.16.cloned.1.call-done, f32[1,512,2048]{2,1,0:T(8,128)} %param.16), kind=kOutput, calls=%fused_computation.79 | convolution fusion | flops 4310695936 | bytes 27262976 | tf_op jit(solution)/shard_map/dot_general | solution.py:116
  427.0 8.4 fusion.89
  435.4 6.1 convolution_add_fusion
  441.6 9.8 convolution_convert_fusion
  451.7 145.0 %all-reduce.13.cloned.1.call-done = f32[512,2048]{1,0:T(8,128)} async-done(((f32[512,2048]{1,0:T(8,128)}), f32[512,2048]{1,0:T(8,128)}) %all-reduce.13.cloned.1.call-update) | async-done | bytes 4194320 | tf_op jit(solution)/shard_map/psum | solution.py:194
  596.7 4.5 multiply_reduce_fusion
  601.2 83.0 %all-reduce.11.cloned.1.call-done = bf16[512,2048]{1,0:T(8,128)(2,1)} async-done(((bf16[512,2048]{1,0:T(8,128)(2,1)}), bf16[512,2048]{1,0:T(8,128)(2,1)}) %all-reduce.11.cloned.1.call-update) | async-done | bytes 2097168 | tf_op jit(solution)/shard_map/psum | solution.py:189
  684.2 8.1 bitcast_add_fusion
  695.6 20.4 %while.27 = (s32[]{:T(128)}, f32[2,4,512,64]{2,3,1,0:T(8,128)}, f32[2,1024,64]{1,2,0:T(8,128)S(1)}, f32[2,1024,64]{1,2,0:T(8,128)}, pred[512,1024]{1,0:T(8,128)(...) while((s32[]{:T(128)}, f32[2,4,512,64]{2,3,1,0:T(8,128)}, ...), condition=%wide.region_12.13_spmd, body=%wide.region_10.12_spmd.sunk | while | flops 1365768192 | bytes 50255028 | solution.py:112
  697.1 3.3 multiply_convert_fusion.7
  702.8 3.1 fusion.170
  707.3 3.3 multiply_convert_fusion.7
  713.0 3.1 fusion.170
  726.8 3.5 fusion.92
  732.2 5.7 fusion.73
  738.0 3.3 fusion.69
  742.9 9.7 fusion.93
  752.7 9.9 fusion.94
  764.1 10.4 fusion.82
  776.4 105.3 %all-reduce.15.cloned.1.call-done = f32[512,2048]{1,0:T(8,128)} async-done(((f32[512,2048]{1,0:T(8,128)}), f32[512,2048]{1,0:T(8,128)}) %all-reduce.15.cloned.1.call-update) | async-done | bytes 4194320 | tf_op jit(solution)/shard_map/psum | solution.py:220
  881.7 4.5 fusion.61
  886.2 24.1 %all-reduce.3 = (f32[2048]{0:T(1024)S(1)}, f32[2048]{0:T(1024)S(1)}) all-reduce(f32[2048]{0:T(1024)S(1)} %get-tuple-element.169, f32[2048]{0:T(1024)S(1)} %get-tuple-element.167), channel_id=9, replica_groups=mesh['fsdp'=4,'ctx'=2,'tp'=4] {'fsdp','ctx'}, use_global_device_ids=true, to_apply=%region_23.24.clone | all-reduce | flops 4096 | bytes 32768
  911.6 7.8 fusion.58
  920.3 39.8 %reduce-scatter.10.cloned.1.call-done = f32[256,128]{1,0:T(8,128)} async-done(((f32[2048,128]{1,0:T(8,128)}), f32[256,128]{1,0:T(8,128)}) %reduce-scatter.10.cloned.1.call-update) | async-done | bytes 131088 | tf_op jit(solution)/shard_map/reduce_scatter | solution.py:225
  960.1 54.9 %reduce-scatter.14.cloned.1.call-done = f32[512,256]{1,0:T(8,128)} async-done(((f32[512,2048]{1,0:T(8,128)}), f32[512,256]{1,0:T(8,128)}) %reduce-scatter.14.cloned.1.call-update) | async-done | bytes 524304 | tf_op jit(solution)/shard_map/reduce_scatter | solution.py:227
  1015.0 55.1 %reduce-scatter.8.cloned.1.call-done = f32[256,512]{1,0:T(8,128)} async-done(((f32[2048,512]{1,0:T(8,128)}), f32[256,512]{1,0:T(8,128)}) %reduce-scatter.8.cloned.1.call-update) | async-done | bytes 524304 | tf_op jit(solution)/shard_map/reduce_scatter | solution.py:224
  1070.1 120.2 %reduce-scatter.16.cloned.1.call-done = f32[256,2048]{1,0:T(8,128)} async-done(((f32[2048,2048]{1,0:T(8,128)}), f32[256,2048]{1,0:T(8,128)}) %reduce-scatter.16.cloned.1.call-update) | async-done | bytes 2097168 | tf_op jit(solution)/shard_map/reduce_scatter | solution.py:228
  1190.3 120.2 %reduce-scatter.18.cloned.1.call-done = f32[256,2048]{1,0:T(8,128)} async-done(((f32[2048,2048]{1,0:T(8,128)}), f32[256,2048]{1,0:T(8,128)}) %reduce-scatter.18.cloned.1.call-update) | async-done | bytes 2097168 | tf_op jit(solution)/shard_map/reduce_scatter | solution.py:229
  1310.5 120.0 %reduce-scatter.20.cloned.1.call-done = f32[2048,256]{1,0:T(8,128)} async-done(((f32[2048,2048]{1,0:T(8,128)}), f32[2048,256]{1,0:T(8,128)}) %reduce-scatter.20.cloned.1.call-update) | async-done | bytes 2097168 | tf_op jit(solution)/shard_map/reduce_scatter | solution.py:230
  (173 shorter events, 61.7 us)
Async XLA Ops:
  7.2 52.1 %all-gather.8.cloned.1.call-start = ((), (), s32[]{:S(2)}) async-start(), calls=%async_computation.7 | async-start | bytes 2359296 | tf_op jit(solution)/shard_map/all_gather | solution.py:133
  7.9 75.1 %all-gather.10.cloned.1.call-start = ((), (), s32[]{:S(2)}) async-start(), calls=%async_computation.8 | async-start | bytes 2359296 | tf_op jit(solution)/shard_map/all_gather | solution.py:136
  19.0 29.3 %copy-start.20 = (f32[8,1,256]{2,1,0:T(1,128)}, f32[8,1,256]{2,1,0:T(1,128)S(1)}, u32[]{:S(2)}) copy-start(f32[8,1,256]{2,1,0:T(1,128)S(1)} %convert_element_type.149) | copy-start | bytes 24580
  29.7 4.8 copy-start.7
  29.9 4.6 copy-start
  33.5 14.8 %copy-start.23 = (f32[512]{0:T(512)}, f32[512]{0:T(512)S(1)}, u32[]{:S(2)}) copy-start(f32[512]{0:T(512)S(1)} %get-tuple-element.236) | copy-start | bytes 6148
  34.5 31.6 %copy-start.13 = (f32[512,32]{0,1:T(8,128)}, f32[512,32]{0,1:T(8,128)S(1)}, u32[]{:S(2)}) copy-start(f32[512,32]{0,1:T(8,128)S(1)} %get-tuple-element.234) | copy-start | bytes 196612
  34.5 4.9 copy-start.22
  34.9 28.2 %copy-start.2 = (bf16[1,512,2048]{2,1,0:T(8,128)(2,1)}, bf16[1,512,2048]{2,1,0:T(8,128)(2,1)S(1)}, u32[]{:S(2)}) copy-start(bf16[1,512,2048]{2,1,0:T(8,128)(2,1)S(1)} %multiply_convert_fusion.5) | copy-start | bytes 6291460
  36.5 18.2 %collective-permute-start = (bf16[512,128]{0,1:T(8,128)(2,1)}, bf16[512,128]{0,1:T(8,128)(2,1)}, u32[]{:S(2)}, u32[]{:S(2)}) collective-permute-start(bf16[512,128]{0,1:T(8,128)(2,1)} %bitcast.31), channel_id=1, source_target_pairs={{0,4},{1,5},{2,6},{3,7},{8,12},{9,13},{10,14},{11,15},{16,20},{17,... | collective-permute-start | bytes 393224 | tf_op jit(solution)/shard_map/ppermute | solution.py:15
  48.3 3.2 copy-start.9
  51.5 4.2 collective-permute-start.1
  54.5 188.6 %all-reduce.9.cloned.1.call-start = ((), (), s32[]{:S(2)}) async-start(), calls=%async_computation.9 | async-start | bytes 8388608 | tf_op jit(solution)/shard_map/psum | solution.py:181
  67.9 2.4 copy-start.18
  74.3 2.4 copy-start.18
  87.9 1.8 copy-start.27
  87.9 210.1 %all-gather.12.cloned.1.call-start = ((), (), s32[]{:S(2)}) async-start(), calls=%async_computation.10 | async-start | bytes 9437184 | tf_op jit(solution)/shard_map/all_gather | solution.py:137
  88.5 265.6 %all-gather.14.cloned.1.call-start = ((), (), s32[]{:S(2)}) async-start(), calls=%async_computation.11 | async-start | bytes 9437184 | tf_op jit(solution)/shard_map/all_gather | solution.py:138
  89.1 322.6 %all-gather.16.cloned.1.call-start = ((), (), s32[]{:S(2)}) async-start(), calls=%async_computation.12 | async-start | bytes 9437184 | tf_op jit(solution)/shard_map/all_gather | solution.py:139
  89.7 507.0 %all-reduce.13.cloned.1.call-start = ((), (), s32[]{:S(2)}) async-start(), calls=%async_computation.14 | async-start | bytes 8388608 | tf_op jit(solution)/shard_map/psum | solution.py:194
  247.0 2.0 copy-start.1
  426.9 8.4 copy-start.30
  426.9 8.4 copy-start.26
  441.6 242.6 %all-reduce.11.cloned.1.call-start = ((), (), s32[]{:S(2)}) async-start(), calls=%async_computation.13 | async-start | bytes 4194304 | tf_op jit(solution)/shard_map/psum | solution.py:189
  451.4 430.3 %all-reduce.15.cloned.1.call-start = ((), (), s32[]{:S(2)}) async-start(), calls=%async_computation.15 | async-start | bytes 8388608 | tf_op jit(solution)/shard_map/psum | solution.py:220
  684.2 10.1 copy-start.12
  692.3 2.0 copy-start.4
  692.3 3.3 copy-start.19
  695.6 24.5 %copy-start.14 = (f32[512,32]{0,1:T(8,128)S(1)}, f32[512,32]{0,1:T(8,128)}, u32[]{:S(2)}) copy-start(f32[512,32]{0,1:T(8,128)} %copy-done.13) | copy-start | bytes 196612
  695.6 24.5 %copy-start.17 = (f32[512,32]{0,1:T(8,128)S(1)}, f32[512,32]{0,1:T(8,128)}, u32[]{:S(2)}) copy-start(f32[512,32]{0,1:T(8,128)} %get-tuple-element.232) | copy-start | bytes 196612
  697.0 3.3 copy-start.15
  707.3 3.3 copy-start.15
  716.1 5.5 copy-start.6
  717.3 6.5 collective-permute-start.3
  718.6 4.3 collective-permute-start.2
  726.8 3.6 copy-start.3
  726.8 193.6 %reduce-scatter.12.cloned.1.call-start = ((), (), s32[]{:S(2)}) async-start(), calls=%async_computation.18 | async-start | bytes 1179648 | tf_op jit(solution)/shard_map/reduce_scatter | solution.py:226
  730.3 229.8 %reduce-scatter.10.cloned.1.call-start = ((), (), s32[]{:S(2)}) async-start(), calls=%async_computation.17 | async-start | bytes 1179648 | tf_op jit(solution)/shard_map/reduce_scatter | solution.py:225
  732.2 282.8 %reduce-scatter.14.cloned.1.call-start = ((), (), s32[]{:S(2)}) async-start(), calls=%async_computation.19 | async-start | bytes 4718592 | tf_op jit(solution)/shard_map/reduce_scatter | solution.py:227
  737.9 332.2 %reduce-scatter.8.cloned.1.call-start = ((), (), s32[]{:S(2)}) async-start(), calls=%async_computation.16 | async-start | bytes 4718592 | tf_op jit(solution)/shard_map/reduce_scatter | solution.py:224
  741.3 1.6 copy-start.11
  741.3 449.0 %reduce-scatter.16.cloned.1.call-start = ((), (), s32[]{:S(2)}) async-start(), calls=%async_computation.20 | async-start | bytes 18874368 | tf_op jit(solution)/shard_map/reduce_scatter | solution.py:228
  752.6 557.9 %reduce-scatter.18.cloned.1.call-start = ((), (), s32[]{:S(2)}) async-start(), calls=%async_computation.21 | async-start | bytes 18874368 | tf_op jit(solution)/shard_map/reduce_scatter | solution.py:229
  762.6 1.6 copy-start.29
  762.6 668.0 %reduce-scatter.20.cloned.1.call-start = ((), (), s32[]{:S(2)}) async-start(), calls=%async_computation.22 | async-start | bytes 18874368 | tf_op jit(solution)/shard_map/reduce_scatter | solution.py:230
  774.5 107.2 %copy-start.21 = (f32[8,1,256]{2,1,0:T(1,128)S(1)}, f32[8,1,256]{2,1,0:T(1,128)}, u32[]{:S(2)}) copy-start(f32[8,1,256]{2,1,0:T(1,128)} %copy-done.20) | copy-start | bytes 24580
  774.6 107.2 %copy-start.24 = (f32[512]{0:T(512)S(1)}, f32[512]{0:T(512)}, u32[]{:S(2)}) copy-start(f32[512]{0:T(512)} %copy-done.23) | copy-start | bytes 6148
  776.4 135.1 %copy-start.25 = (f32[512]{0:T(512)S(1)}, f32[512]{0:T(512)}, u32[]{:S(2)}) copy-start(f32[512]{0:T(512)} %get-tuple-element.235) | copy-start | bytes 6148
  (6 other events, 6.5 us)
Sparse Core Ops, SparseCore 0:
  9.9 31.1 all-gather.7
  54.6 28.3 all-gather.9
  88.0 154.9 all-reduce.8
  244.8 53.2 all-gather.11
  299.8 54.2 all-gather.13
  355.8 55.8 all-gather.15
  441.7 154.9 all-reduce.12
  599.0 85.0 all-reduce.10
  726.9 154.7 all-reduce.14
  885.3 34.9 reduce-scatter.11
  924.1 35.9 reduce-scatter.9
  963.9 51.0 reduce-scatter.13
  1018.9 51.1 reduce-scatter.7
  1074.1 116.1 reduce-scatter.15
  1194.3 116.1 reduce-scatter.17
  1314.5 115.9 reduce-scatter.19
where the time goes:
time: 1450 us; the launch traced here: 1440 us
  waiting for transfers between devices  1130 us (78%)
  matrix products  149 us (10%)
  blocking collectives  63.1 us (4%)
  other arithmetic  46.2 us (3%)
  local copies, waits for them, and re-layouts  19 us (1%)
  between operations  15.6 us (1%)
    psum x1, waiting for transfers between devices, body(): d_hnorm = lax.psum(dotf(d_gate, wg.T) + dotf(d_up, wu.T), 'tp')  145 us
    psum x1, waiting for transfers between devices, body(): hidden = rows + lax.psum(dotf(attn_flat, wo), 'tp')  144 us
    dot_general x21, matrix products, dotf(): return jnp.dot(left, right, preferred_element_type=jnp.float32)  121 us
    reduce_scatter x1, waiting for transfers between devices, body(): lax.psum_scatter(dotf(hnorm.T, d_gate), ('fsdp', 'ctx'), scatter_dimensio...  120 us
    reduce_scatter x1, waiting for transfers between devices, body(): lax.psum_scatter(dotf(hnorm.T, d_up), ('fsdp', 'ctx'), scatter_dimension=...  120 us
    reduce_scatter x1, waiting for transfers between devices, body(): lax.psum_scatter(dotf(inner.T, cot_b), ('fsdp', 'ctx'), scatter_dimension...  120 us
    psum x1, waiting for transfers between devices, body(): lax.psum(dotf(dq_b, wq.T) + dotf(dk_b, wk.T) + dotf(dv_b, wv.T), 'tp')  105 us
    psum x1, waiting for transfers between devices, body(): lax.psum(dotf(inner, wd).astype(jnp.bfloat16), 'tp').astype(jnp.float32)  83 us
  transfers between devices with their start and end apart: 20, of which 15 were waited for; matrix products, arithmetic and copies ran while one was open for 9% of the time, Pallas kernels for 0%

commit v1 on v0

--- a/solution.py
+++ b/solution.py
@@ -7,6 +7,28 @@
 EPS = 1e-05
 BASE = 500000.0
 NEG = -1e30
+
+
+def joined_along(parts, dim):
+    shape = list(parts.shape[1:])
+    shape[dim] *= parts.shape[0]
+    return jnp.moveaxis(parts, 0, dim).reshape(shape)
+
+
+def doubled(shard, axis):
+    size = lax.axis_size(axis)
+    parts = shard[None]
+    for level in range(size.bit_length() - 1):
+        distance = 1 << level
+        partner_block = lax.ppermute(parts, axis, [(i, i ^ distance) for i in range(size)])
+        both = jnp.stack([parts, partner_block])
+        upper = lax.axis_index(axis) >> level & 1
+        parts = jnp.where(upper == 0, both, both[::-1]).reshape(-1, *shard.shape)
+    return parts
+
+
+def doubled_up(x, axis, dim):
+    return joined_along(doubled(x, axis), dim)
 
 
 def shifted(shard, axis, by):
@@ -135,7 +157,7 @@
         lax.all_gather(w_value, ("fsdp", "ctx"), axis=0, tiled=True),
         lax.all_gather(w_output, ("fsdp", "ctx"), axis=1, tiled=True),
         lax.all_gather(w_gate, ("fsdp", "ctx"), axis=0, tiled=True),
-        lax.all_gather(w_up, ("fsdp", "ctx"), axis=0, tiled=True),
+        doubled_up(w_up, ("fsdp", "ctx"), 0),
         lax.all_gather(w_down, ("fsdp", "ctx"), axis=1, tiled=True),
         lax.all_gather(attn_gain, ("fsdp", "ctx"), axis=0, tiled=True),
         lax.all_gather(ffn_gain, ("fsdp", "ctx"), axis=0, tiled=True),

time: 1450 us -> 1400 us (0.966)
  waiting for transfers between devices: 1130 us -> 969 us
  blocking collectives: 63.1 us -> 149 us
  other arithmetic: 46.2 us -> 78.1 us
    psum x1, waiting for transfers between devices: 144 us -> 0.01 us  [body(): hidden = rows + lax.psum(dotf(attn_flat, wo), 'tp')]
    all_gather x1, blocking collectives: 9.09 us -> 95 us  [body(): lax.all_gather(ffn_gain, ('fsdp', 'ctx'), axis=0, tiled=True)]
    ppermute x0 -> x3, waiting for transfers between devices: none -> 49.2 us  [doubled(): lax.ppermute(parts, axis, [(i, i ^ distance) for i in range(size)])]
    all_gather x1 -> x0, waiting for transfers between devices: 45.5 us -> none  [body(): lax.all_gather(w_up, ('fsdp', 'ctx'), axis=0, tiled=True)]
    all_gather x1, waiting for transfers between devices: 47.2 us -> 22 us  [body(): lax.all_gather(w_gate, ('fsdp', 'ctx'), axis=0, tiled=True)]
    select_n x0 -> x2, other arithmetic: none -> 17.4 us  [doubled(): parts = jnp.where(upper == 0, both, both[::-1]).reshape(-1, *shard.shape)]
    another operation x3 -> x7, other arithmetic: 0.17 us -> 14.7 us  [the longest x4 14.5 us: doubled(): both = jnp.stack([parts, partner_block])]
  transfers between devices with their start and end apart: 20 -> 22, of which waited for: 15 -> 15; matrix products, arithmetic and copies ran while one was open for 9% -> 11% of each run, Pallas kernels for 0% -> 0%
where the time goes in v1:
time: 1400 us; the launch traced here: 1390 us
  waiting for transfers between devices  969 us (69%)
  blocking collectives  149 us (11%)
  matrix products  143 us (10%)
  other arithmetic  78.1 us (6%)
  local copies, waits for them, and re-layouts  19 us (1%)
  between operations  15.6 us (1%)
    psum x1, waiting for transfers between devices, body(): d_hnorm = lax.psum(dotf(d_gate, wg.T) + dotf(d_up, wu.T), 'tp')  145 us
    reduce_scatter x1, waiting for transfers between devices, body(): lax.psum_scatter(dotf(hnorm.T, d_gate), ('fsdp', 'ctx'), scatter_dimensio...  120 us
    reduce_scatter x1, waiting for transfers between devices, body(): lax.psum_scatter(dotf(hnorm.T, d_up), ('fsdp', 'ctx'), scatter_dimension=...  120 us
    reduce_scatter x1, waiting for transfers between devices, body(): lax.psum_scatter(dotf(inner.T, cot_b), ('fsdp', 'ctx'), scatter_dimension...  120 us
    dot_general x21, matrix products, dotf(): return jnp.dot(left, right, preferred_element_type=jnp.float32)  115 us
    psum x1, waiting for transfers between devices, body(): lax.psum(dotf(dq_b, wq.T) + dotf(dk_b, wk.T) + dotf(dv_b, wv.T), 'tp')  105 us
    all_gather x1, blocking collectives, body(): lax.all_gather(ffn_gain, ('fsdp', 'ctx'), axis=0, tiled=True)  95 us
    psum x1, waiting for transfers between devices, body(): lax.psum(dotf(inner, wd).astype(jnp.bfloat16), 'tp').astype(jnp.float32)  83.5 us
  transfers between devices with their start and end apart: 22, of which 15 were waited for; matrix products, arithmetic and copies ran while one was open for 11% of the time, Pallas kernels for 0%

profile of v1, /device:TPU:0, one launch (start us, length us, event | category | flops | bytes accessed | tf_op | source)
XLA Modules:
  0.0 1387.2 jit_solution(13115168115154881236)
XLA Ops:
  8.6 10.4 all-gather
  19.0 10.7 all_gather.26
  30.0 3.0 fusion.52
  36.5 2.9 collective-permute-start
  39.4 8.9 all_gather.27
  59.2 3.9 copy.28
  66.3 12.7 while.10
  79.0 4.0 all-gather.9.cloned.1.call-done
  83.0 4.9 fusion.89
  97.8 46.7 %collective-permute-done.3 = bf16[2,256,2048]{2,1,0:T(8,128)(2,1)} collective-permute-done((bf16[2,256,2048]{2,1,0:T(8,128)(2,1)}, bf16[2,256,2048]{2,1,0:T(8,128)(2,1)}, u32[]{:S(2)}, u32[]{:S(2)}) %collective-permute-start.3) | collective-permute-done | bytes 2097184 | tf_op jit(solution)/shard_map/ppermute | solution.py:23
  147.2 3.2 reverse_select_fusion.1
  151.4 95.0 %all-gather.1 = bf16[8,1,256]{2,1,0:T(2,128)(2,1)S(1)} all-gather(bf16[1,1,256]{2,1,0:T(2,128)(2,1)S(1)} %reshape.307), channel_id=1, replica_groups=mesh['fsdp'=4,'ctx'=2,'tp'=4] {'fsdp','ctx'}, dimensions={0}, use_global_device_ids=true | all-gather | bytes 4608 | tf_op jit(solution)/shard_map/all_gather | solution.py:163
  246.4 7.7 pad_maximum_fusion
  254.1 14.2 %reverse_select_fusion = bf16[2,4,256,2048]{3,2,1,0:T(8,128)(2,1)} fusion(bf16[2,4,256,2048]{3,2,1,0:T(8,128)(2,1)} %pad_maximum_fusion, pred[]{:T(512)S(6)} %eq.9), kind=kLoop, calls=%fused_computation.58 | loop fusion | flops 4194304 | bytes 16777216 | tf_op jit(solution)/shard_map/jit(_where)/select_n | solution.py:26
  268.3 4.0 multiply_reduce_fusion.2
  276.1 22.0 %all-gather.11.cloned.1.call-done = bf16[2048,2048]{1,0:T(8,128)(2,1)} async-done(((bf16[256,2048]{1,0:T(8,128)(2,1)}), bf16[2048,2048]{1,0:T(8,128)(2,1)}) %all-gather.11.cloned.1.call-update) | async-done | bytes 8388624 | tf_op jit(solution)/shard_map/all_gather | solution.py:159
  298.1 10.5 fusion.90
  308.6 47.1 %all-gather.13.cloned.1.call-done = bf16[2048,2048]{1,0:T(8,128)(2,1)} async-done(((bf16[2048,256]{1,0:T(8,128)(2,1)}), bf16[2048,2048]{1,0:T(8,128)(2,1)}) %all-gather.13.cloned.1.call-update) | async-done | bytes 8388624 | tf_op jit(solution)/shard_map/all_gather | solution.py:161
  355.7 8.8 fusion.83
  364.5 11.3 multiply_convert_fusion.1
  375.9 8.5 fusion.91
  384.4 6.1 convolution_add_fusion
  390.6 9.8 convolution_convert_fusion
  400.7 145.0 %all-reduce.13.cloned.1.call-done = f32[512,2048]{1,0:T(8,128)} async-done(((f32[512,2048]{1,0:T(8,128)}), f32[512,2048]{1,0:T(8,128)}) %all-reduce.13.cloned.1.call-update) | async-done | bytes 4194320 | tf_op jit(solution)/shard_map/psum | solution.py:216
  545.7 4.5 multiply_reduce_fusion
  550.2 83.5 %all-reduce.11.cloned.1.call-done = bf16[512,2048]{1,0:T(8,128)(2,1)} async-done(((bf16[512,2048]{1,0:T(8,128)(2,1)}), bf16[512,2048]{1,0:T(8,128)(2,1)}) %all-reduce.11.cloned.1.call-update) | async-done | bytes 2097168 | tf_op jit(solution)/shard_map/psum | solution.py:211
  633.7 8.1 bitcast_add_fusion
  645.2 20.4 %while.27 = (s32[]{:T(128)}, f32[2,4,512,64]{2,3,1,0:T(8,128)}, f32[2,1024,64]{1,2,0:T(8,128)S(1)}, f32[2,1024,64]{1,2,0:T(8,128)}, pred[512,1024]{1,0:T(8,128)(...) while((s32[]{:T(128)}, f32[2,4,512,64]{2,3,1,0:T(8,128)}, ...), condition=%wide.region_12.13_spmd, body=%wide.region_10.12_spmd.sunk | while | flops 1365768192 | bytes 50255028 | solution.py:134
  646.6 3.3 multiply_convert_fusion.7
  652.3 3.1 fusion.172
  656.8 3.3 multiply_convert_fusion.7
  662.5 3.1 fusion.172
  676.3 3.5 fusion.94
  681.7 5.7 fusion.75
  687.5 3.3 fusion.69
  692.4 9.7 fusion.95
  702.2 9.9 fusion.96
  713.7 10.4 fusion.85
  726.0 105.3 %all-reduce.15.cloned.1.call-done = f32[512,2048]{1,0:T(8,128)} async-done(((f32[512,2048]{1,0:T(8,128)}), f32[512,2048]{1,0:T(8,128)}) %all-reduce.15.cloned.1.call-update) | async-done | bytes 4194320 | tf_op jit(solution)/shard_map/psum | solution.py:242
  831.3 4.5 fusion.61
  835.8 24.1 %all-reduce.3 = (f32[2048]{0:T(1024)S(1)}, f32[2048]{0:T(1024)S(1)}) all-reduce(f32[2048]{0:T(1024)S(1)} %get-tuple-element.169, f32[2048]{0:T(1024)S(1)} %get-tuple-element.167), channel_id=9, replica_groups=mesh['fsdp'=4,'ctx'=2,'tp'=4] {'fsdp','ctx'}, use_global_device_ids=true, to_apply=%region_23.24.clone | all-reduce | flops 4096 | bytes 32768
  861.1 7.8 fusion.58
  870.0 39.6 %reduce-scatter.10.cloned.1.call-done = f32[256,128]{1,0:T(8,128)} async-done(((f32[2048,128]{1,0:T(8,128)}), f32[256,128]{1,0:T(8,128)}) %reduce-scatter.10.cloned.1.call-update) | async-done | bytes 131088 | tf_op jit(solution)/shard_map/reduce_scatter | solution.py:247
  909.6 55.0 %reduce-scatter.14.cloned.1.call-done = f32[512,256]{1,0:T(8,128)} async-done(((f32[512,2048]{1,0:T(8,128)}), f32[512,256]{1,0:T(8,128)}) %reduce-scatter.14.cloned.1.call-update) | async-done | bytes 524304 | tf_op jit(solution)/shard_map/reduce_scatter | solution.py:249
  964.7 55.0 %reduce-scatter.8.cloned.1.call-done = f32[256,512]{1,0:T(8,128)} async-done(((f32[2048,512]{1,0:T(8,128)}), f32[256,512]{1,0:T(8,128)}) %reduce-scatter.8.cloned.1.call-update) | async-done | bytes 524304 | tf_op jit(solution)/shard_map/reduce_scatter | solution.py:246
  1019.6 120.4 %reduce-scatter.16.cloned.1.call-done = f32[256,2048]{1,0:T(8,128)} async-done(((f32[2048,2048]{1,0:T(8,128)}), f32[256,2048]{1,0:T(8,128)}) %reduce-scatter.16.cloned.1.call-update) | async-done | bytes 2097168 | tf_op jit(solution)/shard_map/reduce_scatter | solution.py:250
  1140.0 120.2 %reduce-scatter.18.cloned.1.call-done = f32[256,2048]{1,0:T(8,128)} async-done(((f32[2048,2048]{1,0:T(8,128)}), f32[256,2048]{1,0:T(8,128)}) %reduce-scatter.18.cloned.1.call-update) | async-done | bytes 2097168 | tf_op jit(solution)/shard_map/reduce_scatter | solution.py:251
  1260.2 120.0 %reduce-scatter.20.cloned.1.call-done = f32[2048,256]{1,0:T(8,128)} async-done(((f32[2048,2048]{1,0:T(8,128)}), f32[2048,256]{1,0:T(8,128)}) %reduce-scatter.20.cloned.1.call-update) | async-done | bytes 2097168 | tf_op jit(solution)/shard_map/reduce_scatter | solution.py:252
  (191 shorter events, 79.5 us)
Async XLA Ops:
  7.2 52.1 %all-gather.7.cloned.1.call-start = ((), (), s32[]{:S(2)}) async-start(), calls=%async_computation.7 | async-start | bytes 2359296 | tf_op jit(solution)/shard_map/all_gather | solution.py:155
  7.9 75.1 %all-gather.9.cloned.1.call-start = ((), (), s32[]{:S(2)}) async-start(), calls=%async_computation.8 | async-start | bytes 2359296 | tf_op jit(solution)/shard_map/all_gather | solution.py:158
  19.0 29.3 %copy-start.22 = (f32[8,1,256]{2,1,0:T(1,128)}, f32[8,1,256]{2,1,0:T(1,128)S(1)}, u32[]{:S(2)}) copy-start(f32[8,1,256]{2,1,0:T(1,128)S(1)} %convert_element_type.149) | copy-start | bytes 24580
  29.7 4.8 copy-start.7
  29.9 4.6 copy-start
  33.5 14.8 %copy-start.25 = (f32[512]{0:T(512)}, f32[512]{0:T(512)S(1)}, u32[]{:S(2)}) copy-start(f32[512]{0:T(512)S(1)} %get-tuple-element.238) | copy-start | bytes 6148
  34.5 31.6 %copy-start.14 = (f32[512,32]{0,1:T(8,128)}, f32[512,32]{0,1:T(8,128)S(1)}, u32[]{:S(2)}) copy-start(f32[512,32]{0,1:T(8,128)S(1)} %get-tuple-element.236) | copy-start | bytes 196612
  34.5 4.9 copy-start.24
  34.9 28.2 %copy-start.2 = (bf16[1,512,2048]{2,1,0:T(8,128)(2,1)}, bf16[1,512,2048]{2,1,0:T(8,128)(2,1)S(1)}, u32[]{:S(2)}) copy-start(bf16[1,512,2048]{2,1,0:T(8,128)(2,1)S(1)} %multiply_convert_fusion.5) | copy-start | bytes 6291460
  36.5 18.2 %collective-permute-start = (bf16[512,128]{0,1:T(8,128)(2,1)}, bf16[512,128]{0,1:T(8,128)(2,1)}, u32[]{:S(2)}, u32[]{:S(2)}) collective-permute-start(bf16[512,128]{0,1:T(8,128)(2,1)} %bitcast.31), channel_id=1, source_target_pairs={{0,4},{1,5},{2,6},{3,7},{8,12},{9,13},{10,14},{11,15},{16,20},{17,... | collective-permute-start | bytes 393224 | tf_op jit(solution)/shard_map/ppermute | solution.py:37
  48.4 3.2 copy-start.9
  51.5 4.2 collective-permute-start.1
  54.5 213.8 %all-reduce.9.cloned.1.call-start = ((), (), s32[]{:S(2)}) async-start(), calls=%async_computation.9 | async-start | bytes 8388608 | tf_op jit(solution)/shard_map/psum | solution.py:203
  74.3 2.4 copy-start.20
  87.9 210.1 %all-gather.11.cloned.1.call-start = ((), (), s32[]{:S(2)}) async-start(), calls=%async_computation.10 | async-start | bytes 9437184 | tf_op jit(solution)/shard_map/all_gather | solution.py:159
  88.5 267.2 %all-gather.13.cloned.1.call-start = ((), (), s32[]{:S(2)}) async-start(), calls=%async_computation.11 | async-start | bytes 9437184 | tf_op jit(solution)/shard_map/all_gather | solution.py:161
  89.1 456.6 %all-reduce.13.cloned.1.call-start = ((), (), s32[]{:S(2)}) async-start(), calls=%async_computation.13 | async-start | bytes 8388608 | tf_op jit(solution)/shard_map/psum | solution.py:216
  89.4 2.9 collective-permute-start.2
  96.5 48.1 %collective-permute-start.3 = (bf16[2,256,2048]{2,1,0:T(8,128)(2,1)}, bf16[2,256,2048]{2,1,0:T(8,128)(2,1)}, u32[]{:S(2)}, u32[]{:S(2)}) collective-permute-start(bf16[2,256,2048]{2,1,0:T(8,128)(2,1)} %get-tuple-element.221), channel_id=1, source_target_pairs={{0,8},{4,12},{8,0},{12,4},{16,24},{20,28},{24,16},{28,20},{1,9},{5... | collective-permute-start | bytes 6291464 | tf_op jit(solution)/shard_map/ppermute | solution.py:23
  147.1 4.3 copy-start.28
  150.3 96.1 %collective-permute-start.4 = (bf16[4,256,2048]{2,1,0:T(8,128)(2,1)}, bf16[4,256,2048]{2,1,0:T(8,128)(2,1)}, u32[]{:S(2)}, u32[]{:S(2)}) collective-permute-start(bf16[4,256,2048]{2,1,0:T(8,128)(2,1)} %bitcast.46), channel_id=1, source_target_pairs={{0,16},{4,20},{8,24},{12,28},{16,0},{20,4},{24,8},{28,12},{1,17},{... | collective-permute-start | bytes 12582920 | tf_op jit(solution)/shard_map/ppermute | solution.py:23
  355.7 8.8 copy-start.11
  355.7 28.7 %slice-start = ((s8[8388608]{0:T(1024)(128)(4,1)}), s8[4194304]{0:T(1024)(128)(4,1)S(1)}, s32[]{:S(2)}) async-start(s8[8388608]{0:T(1024)(128)(4,1)} %bitcast.257), calls=%async_computation.22 | async-start | bytes 8388608
  364.5 19.9 %slice-start.1 = ((s8[8388608]{0:T(1024)(128)(4,1)}), s8[4194304]{0:T(1024)(128)(4,1)S(1)}, s32[]{:S(2)}) async-start(s8[8388608]{0:T(1024)(128)(4,1)} %bitcast.257), calls=%async_computation.23 | async-start | bytes 8388608
  375.9 8.5 copy-start.32
  375.9 8.5 copy-start.31
  390.5 243.2 %all-reduce.11.cloned.1.call-start = ((), (), s32[]{:S(2)}) async-start(), calls=%async_computation.12 | async-start | bytes 4194304 | tf_op jit(solution)/shard_map/psum | solution.py:211
  400.4 430.8 %all-reduce.15.cloned.1.call-start = ((), (), s32[]{:S(2)}) async-start(), calls=%async_computation.14 | async-start | bytes 8388608 | tf_op jit(solution)/shard_map/psum | solution.py:242
  633.7 10.1 copy-start.13
  641.9 3.3 copy-start.21
  645.2 24.5 %copy-start.15 = (f32[512,32]{0,1:T(8,128)S(1)}, f32[512,32]{0,1:T(8,128)}, u32[]{:S(2)}) copy-start(f32[512,32]{0,1:T(8,128)} %copy-done.14) | copy-start | bytes 196612
  645.2 24.5 %copy-start.19 = (f32[512,32]{0,1:T(8,128)S(1)}, f32[512,32]{0,1:T(8,128)}, u32[]{:S(2)}) copy-start(f32[512,32]{0,1:T(8,128)} %get-tuple-element.234) | copy-start | bytes 196612
  646.6 3.3 copy-start.16
  656.8 3.3 copy-start.16
  665.6 5.5 copy-start.6
  666.8 6.5 collective-permute-start.6
  668.2 4.3 collective-permute-start.5
  676.3 3.6 copy-start.3
  676.3 193.7 %reduce-scatter.12.cloned.1.call-start = ((), (), s32[]{:S(2)}) async-start(), calls=%async_computation.17 | async-start | bytes 1179648 | tf_op jit(solution)/shard_map/reduce_scatter | solution.py:248
  679.8 229.8 %reduce-scatter.10.cloned.1.call-start = ((), (), s32[]{:S(2)}) async-start(), calls=%async_computation.16 | async-start | bytes 1179648 | tf_op jit(solution)/shard_map/reduce_scatter | solution.py:247
  681.7 283.0 %reduce-scatter.14.cloned.1.call-start = ((), (), s32[]{:S(2)}) async-start(), calls=%async_computation.18 | async-start | bytes 4718592 | tf_op jit(solution)/shard_map/reduce_scatter | solution.py:249
  687.4 332.2 %reduce-scatter.8.cloned.1.call-start = ((), (), s32[]{:S(2)}) async-start(), calls=%async_computation.15 | async-start | bytes 4718592 | tf_op jit(solution)/shard_map/reduce_scatter | solution.py:246
  690.8 449.2 %reduce-scatter.16.cloned.1.call-start = ((), (), s32[]{:S(2)}) async-start(), calls=%async_computation.19 | async-start | bytes 18874368 | tf_op jit(solution)/shard_map/reduce_scatter | solution.py:250
  702.2 558.1 %reduce-scatter.18.cloned.1.call-start = ((), (), s32[]{:S(2)}) async-start(), calls=%async_computation.20 | async-start | bytes 18874368 | tf_op jit(solution)/shard_map/reduce_scatter | solution.py:251
  712.1 668.1 %reduce-scatter.20.cloned.1.call-start = ((), (), s32[]{:S(2)}) async-start(), calls=%async_computation.21 | async-start | bytes 18874368 | tf_op jit(solution)/shard_map/reduce_scatter | solution.py:252
  724.1 107.2 %copy-start.23 = (f32[8,1,256]{2,1,0:T(1,128)S(1)}, f32[8,1,256]{2,1,0:T(1,128)}, u32[]{:S(2)}) copy-start(f32[8,1,256]{2,1,0:T(1,128)} %copy-done.22) | copy-start | bytes 24580
  724.1 107.2 %copy-start.26 = (f32[512]{0:T(512)S(1)}, f32[512]{0:T(512)}, u32[]{:S(2)}) copy-start(f32[512]{0:T(512)} %copy-done.25) | copy-start | bytes 6148
  726.0 135.1 %copy-start.27 = (f32[512]{0:T(512)S(1)}, f32[512]{0:T(512)}, u32[]{:S(2)}) copy-start(f32[512]{0:T(512)} %get-tuple-element.237) | copy-start | bytes 6148
  (12 other events, 17.5 us)
Sparse Core Ops, SparseCore 0:
  9.9 31.1 all-gather.6
  54.6 28.3 all-gather.8
  88.1 154.9 all-reduce.8
  244.8 53.2 all-gather.10
  299.8 55.8 all-gather.12
  390.7 154.9 all-reduce.12
  548.6 85.0 all-reduce.10
  676.4 154.8 all-reduce.14
  835.0 34.9 reduce-scatter.11
  873.6 35.9 reduce-scatter.9
  913.6 51.0 reduce-scatter.13
  968.4 51.1 reduce-scatter.7
  1023.8 116.1 reduce-scatter.15
  1144.0 116.1 reduce-scatter.17
  1264.2 115.9 reduce-scatter.19
